TPU v7x, 256 devices: a whole 4x4x8 slice. The times are simulated.
256 devices in a mesh: seq: 32 (over x_lo, z, core), wt: 8 (over y, x_hi).
Axes of the slice: x: 4 (x_hi: 2, x_lo: 2; x = x_hi * 2 + x_lo), y: 4, z: 8, core: 2. Of those that a mesh axis runs over, the one named last changes fastest.
Arguments:
- tokens: int32 [8, 4096], P('wt', 'seq'), may hold values from 0 to 511
- embed_table: bfloat16 [512, 8192], P(None, 'wt'), may hold values from -8 to 8
- norm_gain: bfloat16 [8192], P('wt'), may hold values from 0.099609375 to 1.8984375
- w_in: bfloat16 [8192, 3, 4096], P('wt', None, 'seq'), may hold values from -0.0625 to 0.0625
- short_taps: bfloat16 [3, 3, 4096], P(None, None, 'seq'), may hold values from -3 to 3
- filters: bfloat16 [256, 128], P('seq'), may hold values from -2 to 2
- w_out: bfloat16 [8192, 4096], P('wt'), may hold values from -0.09375 to 0.09375
Outputs:
- block_out: bfloat16 [8, 4096, 8192], P(None, 'seq', 'wt')
All inputs are finite; a program needn't handle non-finite values.
Results may differ from a plain program's by a relative error of at most 0.0088.
Values may be sent and summed in bfloat16 or wider, within the bound.
A program may use at most 128 MiB of HBM per device.

v0:
```python
import jax
import jax.numpy as jnp
from jax import lax
from jax.sharding import PartitionSpec as P


def shifted(shard, axis, by):
    size = lax.axis_size(axis)
    pairs = [(i, i + by) for i in range(size) if 0 <= i + by < size]
    return lax.ppermute(shard, axis, pairs)


def causal_pair(filter_vals):
    tap_count = filter_vals.shape[1]
    group_count = filter_vals.shape[0]
    tiled_taps = jnp.tile(filter_vals, (1, 2 * tap_count - 1)).reshape(
        group_count, tap_count, 2 * tap_count - 1
    )[:, :, :tap_count]
    circulant = jnp.swapaxes(tiled_taps, 1, 2)
    row_pos = lax.broadcasted_iota(jnp.int32, (tap_count, tap_count), 0)
    col_pos = lax.broadcasted_iota(jnp.int32, (tap_count, tap_count), 1)
    lower_mask = (row_pos >= col_pos)[None]
    zero_mat = jnp.zeros_like(circulant)
    return (jnp.where(lower_mask, circulant, zero_mat), jnp.where(lower_mask, zero_mat, circulant))


def short_mix(extended, tap_vals):
    row_count = extended.shape[0] - 2
    ext_vals = extended.astype(jnp.float32)
    return (
        tap_vals[0] * ext_vals[2 : 2 + row_count]
        + tap_vals[1] * ext_vals[1 : 1 + row_count]
        + tap_vals[2] * ext_vals[0:row_count]
    )


def run_filter(extended, lower_mat, upper_mat):
    tap_count = lower_mat.shape[1]
    group_count = lower_mat.shape[0]
    chan_count = extended.shape[1]
    blocks = extended.shape[0] // tap_count
    stacked = extended.reshape(blocks, tap_count, group_count, chan_count // group_count)
    filtered = jnp.einsum(
        "gij,bjgc->bigc", lower_mat, stacked[1:], preferred_element_type=jnp.float32
    )
    filtered = filtered + jnp.einsum(
        "gij,bjgc->bigc", upper_mat, stacked[:-1], preferred_element_type=jnp.float32
    )
    return filtered.reshape((blocks - 1) * tap_count, chan_count)


def local(tokens, embed_table, norm_gain, w_in, short_taps, filters, w_out):
    token_ids = tokens[0]
    own_len = token_ids.shape[0]
    tap_count = filters.shape[1]
    table_vals = embed_table.astype(jnp.float32)
    square_sums = lax.psum(jnp.sum(table_vals * table_vals, axis=1, keepdims=True), "wt")
    feature_count = embed_table.shape[1] * lax.axis_size("wt")
    row_scale = lax.rsqrt(square_sums / feature_count + 1e-06)
    normed = (table_vals * row_scale * norm_gain.astype(jnp.float32)).astype(jnp.bfloat16)
    local_chans = w_in.shape[2]
    w_flat = w_in.reshape(w_in.shape[0], 3 * local_chans)
    vocab_size = embed_table.shape[0]
    partial_sum = jnp.dot(normed, w_flat, preferred_element_type=jnp.float32)
    vocab_flat = lax.psum(partial_sum, "wt").astype(jnp.bfloat16)
    vocab_proj = vocab_flat.reshape(vocab_size, 3, local_chans)
    vocab_all, tap_all, filter_all = (
        lax.all_gather(vocab_proj, "seq", axis=2, tiled=True),
        lax.all_gather(short_taps, "seq", axis=2, tiled=True),
        lax.all_gather(filters, "seq", axis=0, tiled=True),
    )
    projected = jnp.take(vocab_all, token_ids, axis=0)
    edge_prev = shifted(projected[own_len - 2 :], "seq", 1)
    mixture = short_mix(
        jnp.concatenate([edge_prev, projected], axis=0), tap_all.astype(jnp.float32)
    )
    product = (mixture[:, 0] * mixture[:, 2]).astype(jnp.bfloat16)
    tail_prev = shifted(product[own_len - tap_count + 1 :], "seq", 1)
    chan_count = product.shape[1]
    extended = jnp.concatenate(
        [jnp.zeros((1, chan_count), jnp.bfloat16), tail_prev, product], axis=0
    )
    lower_mat, upper_mat = causal_pair(filter_all)
    filtered = run_filter(extended, lower_mat, upper_mat)
    gated = (mixture[:, 1] * filtered).astype(jnp.bfloat16)
    everyone = lax.all_gather(tokens, "wt", axis=0, tiled=True)
    branch = jnp.einsum(
        "knc,dc->knd",
        lax.all_gather(gated[None], "wt", axis=0, tiled=True),
        w_out,
        preferred_element_type=jnp.float32,
    )
    embedded = jnp.take(embed_table, everyone, axis=0)
    return (embedded.astype(jnp.float32) + branch).astype(jnp.bfloat16)


def solution(mesh):
    placed = (
        P("wt", "seq"),
        P(None, "wt"),
        P("wt"),
        P("wt", None, "seq"),
        P(None, None, "seq"),
        P("seq", None),
        P("wt", None),
    )
    return jax.shard_map(
        local, mesh=mesh, in_specs=placed, out_specs=P(None, "seq", "wt"), check_vma=False
    )
```

profile of v0, /device:TPU:1, one launch (start us, length us, event | category | flops | bytes accessed | tf_op | source)
XLA Modules:
  0.0 520.0 jit_solution(13024097358544034017)
XLA Ops:
  6.5 1.4 copy.31
  7.9 0.0 copy-start.2
  8.0 0.0 copy-start.4
  8.0 1.5 fusion.4
  9.5 21.6 %psum.14 = f32[512,1]{0,1:T(1,128)S(1)} all-reduce(f32[512,1]{0,1:T(1,128)S(1)} %bitcast.66), channel_id=1, replica_groups=mesh['seq'=32,'wt'=8] {'wt'}, use_global_device_ids=true, to_apply=%region_1.0 | all-reduce | flops 512 | bytes 4096 | tf_op jit(solution)/shard_map/psum | solution.py:57
  31.1 0.7 convert_element_type.45
  31.8 2.0 fusion.12
  33.8 42.2 %all-reduce.2 = bf16[512,384]{1,0:T(8,128)(2,1)S(1)} all-reduce(f32[512,384]{1,0:T(8,128)S(1)} %fusion.12), channel_id=1, replica_groups=mesh['seq'=32,'wt'=8] {'wt'}, use_global_device_ids=true, to_apply=%region_2.0 | all-reduce | flops 196608 | bytes 1179648 | tf_op jit(solution)/shard_map/psum | solution.py:65
  75.9 0.2 copy.32
  76.1 1.1 copy.33
  77.2 0.0 all-gather.4.cloned.1.call-update
  77.2 0.0 all-gather.6.cloned.1.call-start
  77.3 48.3 %all_gather.16 = bf16[3,3,4096]{2,1,0:T(4,128)(2,1)S(1)} all-gather(bf16[3,3,128]{2,1,0:T(4,128)(2,1)S(1)} %copy-done.2), channel_id=1, replica_groups=mesh['seq'=32,'wt'=8] {'seq'}, dimensions={2}, use_global_device_ids=true | all-gather | bytes 76032 | tf_op jit(solution)/shard_map/all_gather | solution.py:69
  125.7 85.9 %all-gather.4.cloned.1.call-done = bf16[512,3,4096]{2,1,0:T(4,128)(2,1)} async-done(((bf16[512,3,128]{2,1,0:T(4,128)(2,1)}), bf16[512,3,4096]{2,1,0:T(4,128)(2,1)}) %all-gather.4.cloned.1.call-update) | async-done | bytes 12582928 | tf_op jit(solution)/shard_map/all_gather | solution.py:68
  211.6 13.3 %gather_fusion.1 = bf16[128,3,4096]{2,1,0:T(4,128)(2,1)} fusion(bf16[512,3,4096]{2,1,0:T(4,128)(2,1)} %all-gather.4.cloned.1.call-done, s32[1024]{0:T(1024)S(1)} %pad_clamp_fusion), kind=kCustom, calls=%fused_computation.1 | custom fusion | bytes 6291968 | tf_op jit(solution)/shard_map/jit(_take)/gather | solution.py:72
  224.9 4.3 broadcast_select_fusion.2
  229.2 2.1 copy-done.1
  231.3 2.2 collective-permute-start
  233.5 31.3 %all_gather.18 = bf16[256,128]{1,0:T(8,128)(2,1)S(1)} all-gather(bf16[8,128]{1,0:T(8,128)(2,1)S(1)} %copy-done.3), channel_id=1, replica_groups=mesh['seq'=32,'wt'=8] {'seq'}, dimensions={0}, use_global_device_ids=true | all-gather | bytes 67584 | tf_op jit(solution)/shard_map/all_gather | solution.py:70
  264.8 0.1 copy.35
  264.9 6.0 %tile.8 = bf16[256,255,128]{0,2,1:T(8,128)(2,1)} broadcast(bf16[256,128]{0,1:T(8,128)(2,1)S(1)} %copy.35), dimensions={0,2} | broadcast | bytes 16777216 | tf_op jit(solution)/shard_map/tile | solution.py:16
  270.9 19.0 %tile.9 = bf16[256,128,255]{0,2,1:T(8,128)(2,1)} reshape(bf16[256,255,128]{0,2,1:T(8,128)(2,1)} %tile.8) | data formatting | bytes 33423360 | tf_op jit(solution)/shard_map/tile | solution.py:16
  289.9 0.0 collective-permute-done
  289.9 4.7 maximum_convert_fusion
  294.6 0.0 slice-start.1
  294.6 0.0 slice-start.2
  294.6 9.4 %fusion = f32[128,3,4096]{2,1,0:T(4,128)} fusion(f32[130,3,4096]{2,1,0:T(4,128)S(1)} %maximum_convert_fusion, f32[3,4096]{1,0:T(4,128)S(1)} %get-tuple-element.8, f32[3,4096]{1,0:T(4,128)S(1)} %get-tuple-element.9, f32[3,4096]{1,0:T(4,128)S(1)} %get-tuple-element.7), kind=kLoop, calls=%fused_computation.4 | loop fusion | flops 7864320 | bytes 25313280 | tf_op jit(solution)/shard_map/add | solution.py:31
  304.0 9.2 %fusion.7 = bf16[128,1,4096]{2,1,0:T(2,128)(2,1)S(1)} fusion(f32[128,3,4096]{2,1,0:T(4,128)} %fusion), kind=kLoop, calls=%fused_computation.21 | loop fusion | flops 1048576 | bytes 5242880 | tf_op jit(solution)/shard_map/convert_element_type | solution.py:77
  313.2 2.1 slice.72
  315.3 2.1 copy.44
  317.4 3.4 collective-permute-start.1
  320.9 6.1 %broadcast_select_fusion = (bf16[256,128,128]{0,1,2:T(8,128)(2,1)}, bf16[256,128,128]{0,1,2:T(8,128)(2,1)}) fusion(pred[128,128]{0,1:T(8,128)(4,1)S(1)} %iota_compare_fusion, bf16[256,128,255]{0,2,1:T(8,128)(2,1)S(1)} %bitcast.57), kind=kLoop, calls=%fused_computation.10 | loop fusion | flops 8388608 | bytes 25182208 | tf_op jit(solution)/shard_map/jit(_where)/select_n | solution.py:24
  327.0 13.5 %copy.36 = bf16[256,128,128]{2,1,0:T(8,128)(2,1)} copy(bf16[256,128,128]{0,1,2:T(8,128)(2,1)} %get-tuple-element.6) | data formatting | bytes 16777216 | tf_op jit(solution)/shard_map/jit(_where)/select_n | solution.py:24
  340.5 13.5 %copy.38 = bf16[256,128,128]{2,1,0:T(8,128)(2,1)} copy(bf16[256,128,128]{0,1,2:T(8,128)(2,1)} %get-tuple-element.5) | data formatting | bytes 16777216 | tf_op jit(solution)/shard_map/jit(_where)/select_n | solution.py:24
  354.0 2.6 copy.34
  356.6 6.8 %fusion.17 = f32[256,16,128]{2,1,0:T(8,128)S(1)} fusion(bf16[128,256,16]{0,2,1:T(8,128)(2,1)S(1)} %bitcast.59, bf16[256,128,128]{2,1,0:T(8,128)(2,1)} %copy.36), kind=kOutput, calls=%fused_computation.43 | convolution fusion | flops 134217728 | bytes 11534336 | tf_op jit(solution)/shard_map/gij,bjgc->bigc/dot_general | solution.py:43
  363.4 1.7 copy.42
  365.1 0.4 concatenate.8.clone
  365.5 9.2 %convolution_add_fusion = f32[256,16,128]{2,1,0:T(8,128)} fusion(f32[256,16,128]{2,1,0:T(8,128)S(1)} %fusion.17, bf16[128,256,16]{0,2,1:T(8,128)(2,1)S(1)} %bitcast.60, bf16[256,128,128]{2,1,0:T(8,128)(2,1)} %copy.38), kind=kOutput, calls=%fused_computation.25 | convolution fusion | flops 134742016 | bytes 13631488 | tf_op jit(solution)/shard_map/gij,bjgc->bigc/dot_general | solution.py:46
  374.6 4.9 copy.39
  379.5 0.0 copy-start
  379.5 6.8 %fusion.9 = bf16[1,128,4096]{2,0,1:T(2,128)(2,1)S(1)} fusion(f32[1,128,4096]{2,0,1:T(1,128)S(1)} %copy.39, f32[128,3,4096]{2,1,0:T(4,128)} %fusion), kind=kLoop, calls=%fused_computation.24 | loop fusion | flops 1048576 | bytes 5242880 | tf_op jit(solution)/shard_map/convert_element_type | solution.py:85
  386.3 2.1 copy.40
  388.4 0.0 all-gather.6.cloned.1.call-update
  388.5 18.6 %all-gather = s32[8,1,128]{2,1,0:T(1,128)S(1)} all-gather(s32[1,1,128]{2,1,0:T(1,128)S(1)} %bitcast.68), channel_id=1, replica_groups=mesh['seq'=32,'wt'=8] {'wt'}, dimensions={0}, use_global_device_ids=true | all-gather | bytes 4608 | tf_op jit(solution)/shard_map/all_gather | solution.py:86
  407.1 4.1 gather_fusion
  411.2 87.3 %all-gather.6.cloned.1.call-done = bf16[8,128,4096]{2,1,0:T(8,128)(2,1)} async-done(((bf16[1,128,4096]{2,1,0:T(8,128)(2,1)}), bf16[8,128,4096]{2,1,0:T(8,128)(2,1)}) %all-gather.6.cloned.1.call-update) | async-done | bytes 8388624 | tf_op jit(solution)/shard_map/all_gather | solution.py:89
  498.5 14.7 %add_convert_fusion = bf16[8,128,1024]{2,1,0:T(8,128)(2,1)} fusion(bf16[8,128,1024]{2,1,0:T(8,128)(2,1)S(1)} %bitcast.61, pred[8,128]{1,0:T(8,128)(4,1)S(1)} %compare_and_fusion, bf16[8,128,4096]{2,1,0:T(8,128)(2,1)} %all-gather.6.cloned.1.call-done, bf16[1024,4096]{1,0:T(8,128)(2,1)} %param.13), kind=kOutput, calls=%fused_computation.13 | convolution fusion | flops 8594128896 | bytes 20972544 | tf_op jit(solution)/shard_map/knc,dc->knd/dot_general | solution.py:87
  (25 shorter events, 0.2 us)
Async XLA Ops:
  6.5 205.1 %all-gather.4.cloned.1.call-start = ((), (), s32[]{:S(2)}) async-start(), calls=%async_computation | async-start | bytes 17301504 | tf_op jit(solution)/shard_map/all_gather | solution.py:68
  7.9 69.3 %copy-start.2 = (bf16[3,3,128]{2,1,0:T(4,128)(2,1)S(1)}, bf16[3,3,128]{2,1,0:T(4,128)(2,1)}, u32[]{:S(2)}) copy-start(bf16[3,3,128]{2,1,0:T(4,128)(2,1)} %param.11) | copy-start | bytes 6916
  8.0 117.6 %copy-start.4 = (s32[1,128]{1,0:T(1,128)S(1)}, s32[1,128]{1,0:T(1,128)}, u32[]{:S(2)}) copy-start(s32[1,128]{1,0:T(1,128)} %param.7) | copy-start | bytes 1540
  77.2 421.3 %all-gather.6.cloned.1.call-start = ((), (), s32[]{:S(2)}) async-start(), calls=%async_computation.1 | async-start | bytes 9437184 | tf_op jit(solution)/shard_map/all_gather | solution.py:89
  224.9 8.6 %copy-start.3 = (bf16[8,128]{1,0:T(8,128)(2,1)S(1)}, bf16[8,128]{1,0:T(8,128)(2,1)}, u32[]{:S(2)}) copy-start(bf16[8,128]{1,0:T(8,128)(2,1)} %param.12) | copy-start | bytes 6148
  229.2 2.1 copy-start.1
  231.3 58.6 %collective-permute-start = (bf16[2,3,4096]{2,1,0:T(4,128)(2,1)S(1)}, bf16[2,3,4096]{2,1,0:T(4,128)(2,1)S(1)}, u32[]{:S(2)}, u32[]{:S(2)}) collective-permute-start(bf16[2,3,4096]{2,1,0:T(4,128)(2,1)S(1)} %slice.62), channel_id=1, source_target_pairs={{0,8},{8,16},{16,24},{24,32},{32,40},{40,48},{48,56},{56,64},{64,7... | collective-permute-start | bytes 147464 | tf_op jit(solution)/shard_map/ppermute | solution.py:10
  294.6 26.3 %slice-start = ((s8[16777216]{0:T(1024)(128)(4,1)}), s8[4194304]{0:T(1024)(128)(4,1)S(1)}, s32[]{:S(2)}) async-start(s8[16777216]{0:T(1024)(128)(4,1)} %bitcast.56), calls=%async_computation.2 | async-start | bytes 8388608
  294.6 26.2 %slice-start.1 = ((s8[16777216]{0:T(1024)(128)(4,1)}), s8[4194304]{0:T(1024)(128)(4,1)S(1)}, s32[]{:S(2)}) async-start(s8[16777216]{0:T(1024)(128)(4,1)} %bitcast.56), calls=%async_computation.3 | async-start | bytes 8388608
  294.6 26.2 %slice-start.2 = ((s8[16777216]{0:T(1024)(128)(4,1)}), s8[4194304]{0:T(1024)(128)(4,1)S(1)}, s32[]{:S(2)}) async-start(s8[16777216]{0:T(1024)(128)(4,1)} %bitcast.56), calls=%async_computation.4 | async-start | bytes 8388608
  304.0 16.9 %slice-start.3 = ((s8[16777216]{0:T(1024)(128)(4,1)}), s8[4194304]{0:T(1024)(128)(4,1)S(1)}, s32[]{:S(2)}) async-start(s8[16777216]{0:T(1024)(128)(4,1)} %bitcast.56), calls=%async_computation.5 | async-start | bytes 8388608
  317.4 45.9 %collective-permute-start.1 = (bf16[127,4096]{1,0:T(8,128)(2,1)}, bf16[127,4096]{1,0:T(8,128)(2,1)}, u32[]{:S(2)}, u32[]{:S(2)}) collective-permute-start(bf16[127,4096]{1,0:T(8,128)(2,1)} %bitcast.55), channel_id=1, source_target_pairs={{0,8},{8,16},{16,24},{24,32},{32,40},{40,48},{48,56},{56,64},{64,7... | collective-permute-start | bytes 3121160 | tf_op jit(solution)/shard_map/ppermute | solution.py:10
  379.5 27.6 %copy-start = (bf16[512,1024]{1,0:T(8,128)(2,1)S(1)}, bf16[512,1024]{1,0:T(8,128)(2,1)}, u32[]{:S(2)}) copy-start(bf16[512,1024]{1,0:T(8,128)(2,1)} %param.8) | copy-start | bytes 3145732
Sparse Core Ops, SparseCore 0:
  77.3 134.2 all-gather.3
  388.6 109.8 all-gather.5
where the time goes:
time: 522 us; the launch traced here: 520 us
  waiting for transfers between devices  173 us (33%)
  blocking collectives  162 us (31%)
  local copies, waits for them, and re-layouts  90.2 us (17%)
  other arithmetic  42.6 us (8%)
  matrix products  32.6 us (6%)
  between operations  13.7 us (3%)
  starting transfers between devices  5.63 us (1%)
    all_gather x1, waiting for transfers between devices, local(): lax.all_gather(gated[None], 'wt', axis=0, tiled=True)  87.3 us
    all_gather x1, waiting for transfers between devices, local(): lax.all_gather(vocab_proj, 'seq', axis=2, tiled=True)  85.9 us
    all_gather x1, blocking collectives, local(): lax.all_gather(short_taps, 'seq', axis=2, tiled=True)  48.3 us
    psum x1, blocking collectives, local(): vocab_flat = lax.psum(partial_sum, 'wt').astype(jnp.bfloat16)  42.2 us
    all_gather x1, blocking collectives, local(): lax.all_gather(filters, 'seq', axis=0, tiled=True)  31.3 us
    another operation x2, local copies, waits for them, and re-layouts, causal_pair(): jnp.tile(filter_vals, (1, 2 * tap_count - 1))  25 us
    psum x1, blocking collectives, local(): lax.psum(jnp.sum(table_vals * table_vals, axis=1, keepdims=True), 'wt')  21.6 us
    all_gather x1, blocking collectives, local(): everyone = lax.all_gather(tokens, 'wt', axis=0, tiled=True)  18.6 us
  transfers between devices with their start and end apart: 4, of which 2 were waited for; matrix products, arithmetic and copies ran while one was open for 14% of the time, Pallas kernels for 0%

commit v1 on v0

--- a/solution.py
+++ b/solution.py
@@ -2,6 +2,7 @@
 import jax.numpy as jnp
 from jax import lax
 from jax.sharding import PartitionSpec as P
+from jax.lax import all_to_all, axis_size
 
 
 def shifted(shard, axis, by):
@@ -65,7 +66,12 @@
     vocab_flat = lax.psum(partial_sum, "wt").astype(jnp.bfloat16)
     vocab_proj = vocab_flat.reshape(vocab_size, 3, local_chans)
     vocab_all, tap_all, filter_all = (
-        lax.all_gather(vocab_proj, "seq", axis=2, tiled=True),
+        jnp.concatenate(
+            all_to_all(
+                jnp.stack([vocab_proj for _ in range(axis_size("seq"))], axis=0), "seq", 0, 0
+            ),
+            axis=2,
+        ),
         lax.all_gather(short_taps, "seq", axis=2, tiled=True),
         lax.all_gather(filters, "seq", axis=0, tiled=True),
     )

time: 522 us -> 750 us (1.44)
  blocking collectives: 162 us -> 415 us
  waiting for transfers between devices: 173 us -> 84.2 us
  local copies, waits for them, and re-layouts: 90.2 us -> 133 us
  starting transfers between devices: 5.63 us -> 25.9 us
    all_gather x1, blocking collectives: 48.3 us -> 305 us  [local(): lax.all_gather(short_taps, 'seq', axis=2, tiled=True)]
    all_gather x1 -> x0, waiting for transfers between devices: 85.9 us -> none  [local(): lax.all_gather(vocab_proj, 'seq', axis=2, tiled=True)]
    reshape x1, local copies, waits for them, and re-layouts: 1.06 us -> 27.5 us  [local(): jnp.concatenate(all_to_all(jnp.stack([vocab_proj for _ in range(axis_size...]
    all_to_all x0 -> x1, starting transfers between devices: none -> 20.1 us  [local(): all_to_all(jnp.stack([vocab_proj for _ in range(axis_size('seq'))], axis=...]
    all_to_all x0 -> x1, local copies, waits for them, and re-layouts: none -> 10.6 us  [local(): all_to_all(jnp.stack([vocab_proj for _ in range(axis_size('seq'))], axis=...]
  transfers between devices with their start and end apart: 4 -> 4, of which waited for: 2 -> 1; matrix products, arithmetic and copies ran while one was open for 14% -> 10% of each run, Pallas kernels for 0% -> 0%
where the time goes in v1:
time: 750 us; the launch traced here: 748 us
  blocking collectives  415 us (55%)
  local copies, waits for them, and re-layouts  133 us (18%)
  waiting for transfers between devices  84.2 us (11%)
  other arithmetic  42.7 us (6%)
  matrix products  32.6 us (4%)
  starting transfers between devices  25.9 us (3%)
  between operations  13.7 us (2%)
    all_gather x1, blocking collectives, local(): lax.all_gather(short_taps, 'seq', axis=2, tiled=True)  305 us
    all_gather x1, waiting for transfers between devices, local(): lax.all_gather(gated[None], 'wt', axis=0, tiled=True)  84.2 us
    psum x1, blocking collectives, local(): vocab_flat = lax.psum(partial_sum, 'wt').astype(jnp.bfloat16)  42.2 us
    all_gather x1, blocking collectives, local(): lax.all_gather(filters, 'seq', axis=0, tiled=True)  31.1 us
    reshape x1, local copies, waits for them, and re-layouts, local(): jnp.concatenate(all_to_all(jnp.stack([vocab_proj for _ in range(axis_size...  27.5 us
    another operation x2, local copies, waits for them, and re-layouts, causal_pair(): jnp.tile(filter_vals, (1, 2 * tap_count - 1))  25 us
    psum x1, blocking collectives, local(): lax.psum(jnp.sum(table_vals * table_vals, axis=1, keepdims=True), 'wt')  21.6 us
    all_to_all x1, starting transfers between devices, local(): all_to_all(jnp.stack([vocab_proj for _ in range(axis_size('seq'))], axis=...  20.1 us
  transfers between devices with their start and end apart: 4, of which 1 were waited for; matrix products, arithmetic and copies ran while one was open for 10% of the time, Pallas kernels for 0%

profile of v1, /device:TPU:1, one launch (start us, length us, event | category | flops | bytes accessed | tf_op | source)
XLA Modules:
  0.0 747.5 jit_solution(9348995799365702396)
XLA Ops:
  6.5 1.4 copy.32
  7.9 1.5 fusion.4
  9.4 21.6 %psum.14 = f32[512,1]{0,1:T(1,128)S(1)} all-reduce(f32[512,1]{0,1:T(1,128)S(1)} %bitcast.70), channel_id=1, replica_groups=mesh['seq'=32,'wt'=8] {'wt'}, use_global_device_ids=true, to_apply=%region_1.0 | all-reduce | flops 512 | bytes 4096 | tf_op jit(solution)/shard_map/psum | solution.py:58
  31.0 0.7 convert_element_type.45
  31.7 2.0 fusion.12
  33.7 42.2 %all-reduce.2 = bf16[512,384]{1,0:T(8,128)(2,1)S(1)} all-reduce(f32[512,384]{1,0:T(8,128)S(1)} %fusion.12), channel_id=1, replica_groups=mesh['seq'=32,'wt'=8] {'wt'}, use_global_device_ids=true, to_apply=%region_2.0 | all-reduce | flops 196608 | bytes 1179648 | tf_op jit(solution)/shard_map/psum | solution.py:66
  75.9 0.2 copy.33
  76.1 6.0 stack.3
  82.1 20.1 %all-to-all-start = ((bf16[32,512,3,128]{1,3,2,0:T(8,128)(2,1)}), bf16[32,512,3,128]{1,3,2,0:T(8,128)(2,1)}, u32[]{:S(2)}, u32[]{:S(2)}) async-start(bf16[32,512,3,128]{1,3,2,0:T(8,128)(2,1)} %stack.3), calls=%async_computation | async-start | bytes 25165824 | tf_op jit(solution)/shard_map/all_to_all | solution.py:70
  102.2 0.0 all-gather.3.cloned.1.call-start
  102.3 304.6 %all_gather.13 = bf16[3,3,4096]{2,1,0:T(4,128)(2,1)S(1)} all-gather(bf16[3,3,128]{2,1,0:T(4,128)(2,1)S(1)} %copy-done.2), channel_id=1, replica_groups=mesh['seq'=32,'wt'=8] {'seq'}, dimensions={2}, use_global_device_ids=true | all-gather | bytes 76032 | tf_op jit(solution)/shard_map/all_gather | solution.py:75
  407.0 0.0 all-to-all-done
  407.0 10.6 %copy.34 = bf16[32,512,3,128]{1,3,0,2:T(8,128)(2,1)} copy(bf16[32,512,3,128]{1,3,2,0:T(8,128)(2,1)} %all-to-all-done) | data formatting | bytes 25165824 | tf_op jit(solution)/shard_map/all_to_all | solution.py:70
  417.6 27.5 %copy.35 = bf16[512,3,4096]{2,1,0:T(4,128)(2,1)} copy(bf16[512,3,4096]{0,2,1:T(8,128)(2,1)} %bitcast.59) | data formatting | bytes 25165824 | tf_op jit(solution)/shard_map/reshape | solution.py:69
  445.1 13.3 %gather_fusion.1 = bf16[128,3,4096]{2,1,0:T(4,128)(2,1)} fusion(bf16[512,3,4096]{2,1,0:T(4,128)(2,1)} %copy.35, s32[1024]{0:T(1024)S(1)} %pad_clamp_fusion), kind=kCustom, calls=%fused_computation.1 | custom fusion | bytes 6291968 | tf_op jit(solution)/shard_map/jit(_take)/gather | solution.py:78
  458.4 4.3 broadcast_select_fusion.2
  462.7 2.1 copy-done.1
  464.8 1.9 collective-permute-start
  466.7 31.1 %all_gather.14 = bf16[256,128]{1,0:T(8,128)(2,1)S(1)} all-gather(bf16[8,128]{1,0:T(8,128)(2,1)S(1)} %copy-done.3), channel_id=1, replica_groups=mesh['seq'=32,'wt'=8] {'seq'}, dimensions={0}, use_global_device_ids=true | all-gather | bytes 67584 | tf_op jit(solution)/shard_map/all_gather | solution.py:76
  497.8 0.1 copy.37
  497.9 5.9 tile.8
  503.8 19.0 %tile.9 = bf16[256,128,255]{0,2,1:T(8,128)(2,1)} reshape(bf16[256,255,128]{0,2,1:T(8,128)(2,1)} %tile.8) | data formatting | bytes 33423360 | tf_op jit(solution)/shard_map/tile | solution.py:17
  522.9 0.0 collective-permute-done
  522.9 4.7 maximum_convert_fusion
  527.5 0.0 slice-start
  527.5 0.0 slice-start.1
  527.6 9.4 %fusion = f32[128,3,4096]{2,1,0:T(4,128)} fusion(f32[130,3,4096]{2,1,0:T(4,128)S(1)} %maximum_convert_fusion, f32[3,4096]{1,0:T(4,128)S(1)} %get-tuple-element.8, f32[3,4096]{1,0:T(4,128)S(1)} %get-tuple-element.9, f32[3,4096]{1,0:T(4,128)S(1)} %get-tuple-element.7), kind=kLoop, calls=%fused_computation.4 | loop fusion | flops 7864320 | bytes 25313280 | tf_op jit(solution)/shard_map/add | solution.py:32
  537.0 9.2 %fusion.7 = bf16[128,1,4096]{2,1,0:T(2,128)(2,1)S(1)} fusion(f32[128,3,4096]{2,1,0:T(4,128)} %fusion), kind=kLoop, calls=%fused_computation.21 | loop fusion | flops 1048576 | bytes 5242880 | tf_op jit(solution)/shard_map/convert_element_type | solution.py:83
  546.2 2.1 slice.72
  548.4 2.1 copy.46
  550.5 3.9 collective-permute-start.1
  554.4 6.1 broadcast_select_fusion
  560.5 13.5 %copy.38 = bf16[256,128,128]{2,1,0:T(8,128)(2,1)} copy(bf16[256,128,128]{0,1,2:T(8,128)(2,1)} %get-tuple-element.6) | data formatting | bytes 16777216 | tf_op jit(solution)/shard_map/jit(_where)/select_n | solution.py:25
  574.0 13.5 %copy.40 = bf16[256,128,128]{2,1,0:T(8,128)(2,1)} copy(bf16[256,128,128]{0,1,2:T(8,128)(2,1)} %get-tuple-element.5) | data formatting | bytes 16777216 | tf_op jit(solution)/shard_map/jit(_where)/select_n | solution.py:25
  587.5 2.6 copy.36
  590.1 6.8 fusion.17
  596.9 1.7 copy.44
  598.6 0.4 concatenate.8.clone
  599.0 9.2 %convolution_add_fusion = f32[256,16,128]{2,1,0:T(8,128)} fusion(f32[256,16,128]{2,1,0:T(8,128)S(1)} %fusion.17, bf16[128,256,16]{0,2,1:T(8,128)(2,1)S(1)} %bitcast.64, bf16[256,128,128]{2,1,0:T(8,128)(2,1)} %copy.40), kind=kOutput, calls=%fused_computation.25 | convolution fusion | flops 134742016 | bytes 13631488 | tf_op jit(solution)/shard_map/gij,bjgc->bigc/dot_general | solution.py:47
  608.2 4.9 copy.41
  613.0 0.0 copy-start
  613.0 6.8 fusion.9
  619.8 2.1 copy.42
  621.9 0.0 all-gather.3.cloned.1.call-update
  622.0 15.7 %all-gather = s32[8,1,128]{2,1,0:T(1,128)S(1)} all-gather(s32[1,1,128]{2,1,0:T(1,128)S(1)} %bitcast.72), channel_id=1, replica_groups=mesh['seq'=32,'wt'=8] {'wt'}, dimensions={0}, use_global_device_ids=true | all-gather | bytes 4608 | tf_op jit(solution)/shard_map/all_gather | solution.py:92
  637.7 4.1 gather_fusion
  641.8 84.2 %all-gather.3.cloned.1.call-done = bf16[8,128,4096]{2,1,0:T(8,128)(2,1)} async-done(((bf16[1,128,4096]{2,1,0:T(8,128)(2,1)}), bf16[8,128,4096]{2,1,0:T(8,128)(2,1)}) %all-gather.3.cloned.1.call-update) | async-done | bytes 8388624 | tf_op jit(solution)/shard_map/all_gather | solution.py:95
  726.0 14.7 %add_convert_fusion = bf16[8,128,1024]{2,1,0:T(8,128)(2,1)} fusion(bf16[8,128,1024]{2,1,0:T(8,128)(2,1)S(1)} %bitcast.65, pred[8,128]{1,0:T(8,128)(4,1)S(1)} %compare_and_fusion, bf16[8,128,4096]{2,1,0:T(8,128)(2,1)} %all-gather.3.cloned.1.call-done, bf16[1024,4096]{1,0:T(8,128)(2,1)} %param.13), kind=kOutput, calls=%fused_computation.13 | convolution fusion | flops 8594128896 | bytes 20972544 | tf_op jit(solution)/shard_map/knc,dc->knd/dot_general | solution.py:93
  (26 shorter events, 0.2 us)
Async XLA Ops:
  82.1 20.1 %copy-start.2 = (bf16[3,3,128]{2,1,0:T(4,128)(2,1)S(1)}, bf16[3,3,128]{2,1,0:T(4,128)(2,1)}, u32[]{:S(2)}) copy-start(bf16[3,3,128]{2,1,0:T(4,128)(2,1)} %param.11) | copy-start | bytes 6916
  82.1 324.8 %copy-start.4 = (s32[1,128]{1,0:T(1,128)S(1)}, s32[1,128]{1,0:T(1,128)}, u32[]{:S(2)}) copy-start(s32[1,128]{1,0:T(1,128)} %param.7) | copy-start | bytes 1540
  82.1 324.9 %all-to-all-start = ((bf16[32,512,3,128]{1,3,2,0:T(8,128)(2,1)}), bf16[32,512,3,128]{1,3,2,0:T(8,128)(2,1)}, u32[]{:S(2)}, u32[]{:S(2)}) async-start(bf16[32,512,3,128]{1,3,2,0:T(8,128)(2,1)} %stack.3), calls=%async_computation | async-start | bytes 25165824 | tf_op jit(solution)/shard_map/all_to_all | solution.py:70
  102.2 623.8 %all-gather.3.cloned.1.call-start = ((), (), s32[]{:S(2)}) async-start(), calls=%async_computation.1 | async-start | bytes 9437184 | tf_op jit(solution)/shard_map/all_gather | solution.py:95
  458.4 8.3 %copy-start.3 = (bf16[8,128]{1,0:T(8,128)(2,1)S(1)}, bf16[8,128]{1,0:T(8,128)(2,1)}, u32[]{:S(2)}) copy-start(bf16[8,128]{1,0:T(8,128)(2,1)} %param.12) | copy-start | bytes 6148
  462.7 2.1 copy-start.1
  464.8 58.1 %collective-permute-start = (bf16[2,3,4096]{2,1,0:T(4,128)(2,1)S(1)}, bf16[2,3,4096]{2,1,0:T(4,128)(2,1)S(1)}, u32[]{:S(2)}, u32[]{:S(2)}) collective-permute-start(bf16[2,3,4096]{2,1,0:T(4,128)(2,1)S(1)} %slice.62), channel_id=1, source_target_pairs={{0,8},{8,16},{16,24},{24,32},{32,40},{40,48},{48,56},{56,64},{64,7... | collective-permute-start | bytes 147464 | tf_op jit(solution)/shard_map/ppermute | solution.py:11
  527.5 26.8 %slice-start = ((s8[16777216]{0:T(1024)(128)(4,1)}), s8[4194304]{0:T(1024)(128)(4,1)S(1)}, s32[]{:S(2)}) async-start(s8[16777216]{0:T(1024)(128)(4,1)} %bitcast.60), calls=%async_computation.2 | async-start | bytes 8388608
  527.5 26.8 %slice-start.1 = ((s8[16777216]{0:T(1024)(128)(4,1)}), s8[4194304]{0:T(1024)(128)(4,1)S(1)}, s32[]{:S(2)}) async-start(s8[16777216]{0:T(1024)(128)(4,1)} %bitcast.60), calls=%async_computation.3 | async-start | bytes 8388608
  527.6 26.8 %slice-start.2 = ((s8[16777216]{0:T(1024)(128)(4,1)}), s8[4194304]{0:T(1024)(128)(4,1)S(1)}, s32[]{:S(2)}) async-start(s8[16777216]{0:T(1024)(128)(4,1)} %bitcast.60), calls=%async_computation.4 | async-start | bytes 8388608
  537.0 17.4 %slice-start.3 = ((s8[16777216]{0:T(1024)(128)(4,1)}), s8[4194304]{0:T(1024)(128)(4,1)S(1)}, s32[]{:S(2)}) async-start(s8[16777216]{0:T(1024)(128)(4,1)} %bitcast.60), calls=%async_computation.5 | async-start | bytes 8388608
  550.5 46.4 %collective-permute-start.1 = (bf16[127,4096]{1,0:T(8,128)(2,1)}, bf16[127,4096]{1,0:T(8,128)(2,1)}, u32[]{:S(2)}, u32[]{:S(2)}) collective-permute-start(bf16[127,4096]{1,0:T(8,128)(2,1)} %bitcast.58), channel_id=1, source_target_pairs={{0,8},{8,16},{16,24},{24,32},{32,40},{40,48},{48,56},{56,64},{64,7... | collective-permute-start | bytes 3121160 | tf_op jit(solution)/shard_map/ppermute | solution.py:11
  613.0 24.7 %copy-start = (bf16[512,1024]{1,0:T(8,128)(2,1)S(1)}, bf16[512,1024]{1,0:T(8,128)(2,1)}, u32[]{:S(2)}) copy-start(bf16[512,1024]{1,0:T(8,128)(2,1)} %param.8) | copy-start | bytes 3145732
Sparse Core Ops, SparseCore 0:
  622.1 103.8 all-gather.2
